TPU v7x, 32 devices: a whole 2x2x4 slice. The times are simulated.
32 devices in a mesh: seq: 8 (over z, y), head: 4 (over x, core).
Axes of the slice: x: 2, y: 2, z: 4, core: 2. Of those that a mesh axis runs over, the one named last changes fastest.
Arguments:
- block_in: bfloat16 [1, 2048, 1024], P(None, 'seq'), may hold values from -6 to 6
- upstream: bfloat16 [1, 2048, 1024], P(None, 'seq'), may hold values from -6 to 6
- first_gain: float32 [1024], replicated, may hold values from 0.5 to 1.5
- project_in: bfloat16 [1024, 4, 512], P(None, 'head'), may hold values from -0.1875 to 0.1875
- filter_taps: float32 [4, 4, 512], P(None, 'head'), may hold values from -2 to 2
- squeeze: bfloat16 [1024, 16], replicated, may hold values from -0.1875 to 0.1875
- expand: bfloat16 [16, 512], P(None, 'head'), may hold values from -0.75 to 0.75
- decay_bias: float32 [512], P('head'), may hold values from 0 to 16
- gating: bfloat16 [1024, 1024], P(None, 'head'), may hold values from -0.1875 to 0.1875
- head_scale: float32 [256], replicated, may hold values from 0.5 to 1.5
- project_out: bfloat16 [1024, 1024], P('head'), may hold values from -0.375 to 0.375
- second_gain: float32 [1024], replicated, may hold values from 0.5 to 1.5
- hidden_gate: bfloat16 [1024, 2816], P(None, 'head'), may hold values from -0.1875 to 0.1875
- hidden_lift: bfloat16 [1024, 2816], P(None, 'head'), may hold values from -0.1875 to 0.1875
- hidden_drop: bfloat16 [2816, 1024], P('head'), may hold values from -0.15625 to 0.15625
Outputs:
- block_out: bfloat16 [1, 2048, 1024], P(None, 'seq')
- input_grad: float32 [1, 2048, 1024], P(None, 'seq')
- grad_first: float32 [1024], replicated
- grad_project: float32 [1024, 4, 512], P('seq', 'head')
- grad_taps: float32 [4, 4, 512], P(None, 'head')
- grad_squeeze: float32 [1024, 16], replicated
- grad_expand: float32 [16, 512], P(None, 'head')
- grad_bias: float32 [512], P('head')
- grad_gating: float32 [1024, 1024], P('seq', 'head')
- grad_scale: float32 [256], replicated
- grad_output: float32 [1024, 1024], P('head', 'seq')
- grad_second: float32 [1024], replicated
- grad_gate: float32 [1024, 2816], P('seq', 'head')
- grad_lift: float32 [1024, 2816], P('seq', 'head')
- grad_drop: float32 [2816, 1024], P('head', 'seq')
All inputs are finite; a program needn't handle non-finite values.
Results may differ from a plain program's by a relative error of at most 0.02.
Values sent between devices are 32-bit elements; how exact they have to be, the bound alone decides.
A program may use at most 128 MiB of HBM per device.

v0:
```python
import jax
import jax.numpy as jnp
from jax import lax
from jax.sharding import PartitionSpec as P

GROUP = 64
EPS = 1e-05
NORMALIZER = 16.0
HIGH = lax.Precision.HIGHEST


def shifted(x, axis, by):
    size = lax.axis_size(axis)
    pairs = [(i, i + by) for i in range(size) if 0 <= i + by < size]
    return lax.ppermute(x, axis, pairs)


def entering(value, axis, join, neutral, backward):
    count, mine = (lax.axis_size(axis), lax.axis_index(axis))
    pieces = jax.tree.map(lambda part: lax.all_gather(part, axis), value)
    if backward:
        pieces = jax.tree.map(lambda part: part[::-1], pieces)
        mine = count - 1 - mine
    total = jax.tree.map(
        lambda part, zero: jnp.full_like(part, 0) + jnp.asarray(zero, part.dtype), value, neutral
    )

    def lap(position, total):
        longer = join(total, jax.tree.map(lambda part: part[position], pieces))
        return jax.tree.map(lambda new, old: jnp.where(position < mine, new, old), longer, total)

    return lax.fori_loop(0, count - 1, lap, total)


def product(left, right):
    return jnp.dot(left, right, preferred_element_type=jnp.float32)


def against(left, right):
    return lax.dot_general(
        left, right, (((1,), (1,)), ((), ())), preferred_element_type=jnp.float32
    )


def across(left, right):
    return lax.dot_general(
        left, right, (((0,), (0,)), ((), ())), preferred_element_type=jnp.float32
    )


def rms_scale(values):
    return lax.rsqrt(jnp.mean(values * values, axis=-1, keepdims=True) + EPS)


def rms_back(values, scale, gain, incoming):
    weighted = gain * incoming
    cube = scale * scale * scale
    return scale * weighted - values * cube * jnp.mean(values * weighted, axis=-1, keepdims=True)


def silu_grad(values):
    logistic = jax.nn.sigmoid(values)
    return logistic * (1.0 + values * (1.0 - logistic))


def causal_mask(size):
    rows = lax.broadcasted_iota(jnp.int32, (size, size), 0)
    columns = lax.broadcasted_iota(jnp.int32, (size, size), 1)
    return (columns <= rows).astype(jnp.float32)


def chain(earlier, later):
    return (earlier[0] * later[0], later[0][..., None] * earlier[1] + later[1])


def grouped(array, seqs, count):
    return array.reshape((seqs, count, GROUP) + array.shape[2:])


def local_states(decays, updates, backward):

    def step(carry, item):
        decay, update = item
        return (jnp.exp(decay)[..., None] * carry + update, carry)

    init = jnp.zeros_like(updates[:, 0])
    total, states = lax.scan(
        step, init, (jnp.moveaxis(decays, 1, 0), jnp.moveaxis(updates, 1, 0)), reverse=backward
    )
    return (jnp.moveaxis(states, 0, 1), total)


def body(
    block_in,
    upstream,
    first_gain,
    project_in,
    filter_taps,
    squeeze,
    expand,
    decay_bias,
    gating,
    head_scale,
    project_out,
    second_gain,
    hidden_gate,
    hidden_lift,
    hidden_drop,
):
    seqs, tokens, width = block_in.shape
    total_rows = seqs * tokens
    key_dim = expand.shape[1]
    value_dim = gating.shape[1]
    mixed_dim = project_in.shape[2]
    lags = filter_taps.shape[0] - 1
    count = tokens // GROUP
    taps = filter_taps.reshape(lags + 1, mixed_dim)
    weight_in = project_in.reshape(width, mixed_dim)
    residual_in = block_in.reshape(total_rows, width).astype(jnp.float32)
    scale_one = rms_scale(residual_in)
    normed_one = (residual_in * scale_one * first_gain).astype(jnp.bfloat16)
    projected = product(normed_one, weight_in).reshape(seqs, tokens, mixed_dim)
    before = shifted(projected[:, tokens - lags :], "seq", 1)
    padded = jnp.concatenate([before, projected], axis=1)
    filtered = taps[0] * projected
    for lag in range(1, lags + 1):
        filtered = filtered + taps[lag] * padded[:, lags - lag : lags - lag + tokens]
    activated_low = jax.nn.silu(filtered).astype(jnp.bfloat16)
    activated = lax.optimization_barrier(activated_low).astype(jnp.float32)
    root = key_dim ** (-0.5)
    query = grouped(activated[..., :key_dim] * root, seqs, count)
    keys = grouped(activated[..., key_dim : 2 * key_dim], seqs, count)
    values = grouped(activated[..., 2 * key_dim :], seqs, count)
    squeezed = product(normed_one, squeeze).astype(jnp.bfloat16)
    logits = product(squeezed, expand) + decay_bias
    log_decay = grouped(
        (jax.nn.log_sigmoid(logits) / NORMALIZER).reshape(seqs, tokens, key_dim), seqs, count
    )
    gate_in = product(normed_one, gating)
    mask = causal_mask(GROUP)
    running = jnp.einsum("ij,snjc->snic", mask, log_decay, precision=HIGH)
    last = running[:, :, -1]
    query_in = query * jnp.exp(running)
    key_in = keys * jnp.exp(-running)
    key_end = keys * jnp.exp(last[:, :, None] - running)
    scores = jnp.einsum("snic,snjc->snij", query_in, key_in, precision=HIGH) * mask
    updates = jnp.einsum("snjc,snjd->sncd", key_end, values, precision=HIGH)
    starts_zero, state_total = local_states(last, updates, False)
    decay_sum = jnp.sum(last, axis=1)
    decay_total = jnp.exp(decay_sum)
    identity = (jnp.ones_like(decay_total), jnp.zeros_like(state_total))
    incoming = entering((decay_total, state_total), "seq", chain, identity, False)[1]
    before_group = jnp.cumsum(last, axis=1) - last
    starts = starts_zero + jnp.exp(before_group)[..., None] * incoming[:, None]
    mixed = jnp.einsum("snij,snjd->snid", scores, values, precision=HIGH)
    mixed = mixed + jnp.einsum("snic,sncd->snid", query_in, starts, precision=HIGH)
    mixed = mixed.reshape(total_rows, value_dim)
    scale_head = rms_scale(mixed)
    normed_head = mixed * scale_head * head_scale
    gated = (normed_head * jax.nn.silu(gate_in)).astype(jnp.bfloat16)
    branch = lax.psum(product(gated, project_out), "head")
    residual = residual_in + branch
    scale_two = rms_scale(residual)
    normed_two = (residual * scale_two * second_gain).astype(jnp.bfloat16)
    gate_value = product(normed_two, hidden_gate)
    lift_value = product(normed_two, hidden_lift)
    inner = (jax.nn.silu(gate_value) * lift_value).astype(jnp.bfloat16)
    feed = lax.psum(product(inner, hidden_drop), "head")
    block_out = (residual + feed).astype(jnp.bfloat16).reshape(seqs, tokens, width)
    seed = upstream.reshape(total_rows, width)
    grad_drop = across(inner, seed)
    grad_inner = against(seed, hidden_drop)
    grad_gv = (grad_inner * lift_value * silu_grad(gate_value)).astype(jnp.bfloat16)
    grad_lv = (grad_inner * jax.nn.silu(gate_value)).astype(jnp.bfloat16)
    grad_gate = across(normed_two, grad_gv)
    grad_lift = across(normed_two, grad_lv)
    feed_grads = (
        lax.psum_scatter(grad_gate, "seq", scatter_dimension=0, tiled=True),
        lax.psum_scatter(grad_lift, "seq", scatter_dimension=0, tiled=True),
        lax.psum_scatter(grad_drop, "seq", scatter_dimension=1, tiled=True),
    )
    grad_two = lax.psum(against(grad_gv, hidden_gate) + against(grad_lv, hidden_lift), "head")
    grad_second = jnp.sum(grad_two * residual * scale_two, axis=0)
    grad_resid = seed.astype(jnp.float32) + rms_back(residual, scale_two, second_gain, grad_two)
    resid_low = grad_resid.astype(jnp.bfloat16)
    grad_output = across(gated, resid_low)
    grad_gated = against(resid_low, project_out)
    grad_gatein = (grad_gated * normed_head * silu_grad(gate_in)).astype(jnp.bfloat16)
    grad_normhead = grad_gated * jax.nn.silu(gate_in)
    grad_scale = jnp.sum(grad_normhead * mixed * scale_head, axis=0)
    grad_mixed_low = rms_back(mixed, scale_head, head_scale, grad_normhead).astype(jnp.bfloat16)
    grad_mixed = lax.optimization_barrier(grad_mixed_low).astype(jnp.float32)
    outgrad = grouped(grad_mixed.reshape(seqs, tokens, value_dim), seqs, count)
    query_end = jnp.einsum("snic,snid->sncd", query_in, outgrad, precision=HIGH)
    following_zero, back_total = local_states(last, query_end, True)
    after = entering((decay_total, back_total), "seq", chain, identity, True)[1]
    after_group = decay_sum[:, None] - jnp.cumsum(last, axis=1)
    following = following_zero + jnp.exp(after_group)[..., None] * after[:, None]
    inner_group = jnp.einsum("snid,snjd->snij", outgrad, values, precision=HIGH) * mask
    grad_query = jnp.exp(running) * (
        jnp.einsum("snij,snjc->snic", inner_group, key_in, precision=HIGH)
        + jnp.einsum("snid,sncd->snic", outgrad, starts, precision=HIGH)
    )
    grad_keys = jnp.exp(-running) * jnp.einsum(
        "snij,snic->snjc", inner_group, query_in, precision=HIGH
    )
    grad_keys = grad_keys + jnp.exp(last[:, :, None] - running) * jnp.einsum(
        "snjd,sncd->snjc", values, following, precision=HIGH
    )
    grad_values = jnp.einsum("snij,snid->snjd", scores, outgrad, precision=HIGH)
    grad_values = grad_values + jnp.einsum("snjc,sncd->snjd", key_end, following, precision=HIGH)
    grad_running = (query * grad_query - keys * grad_keys).reshape(seqs, tokens, key_dim)
    state_end = decay_total[..., None] * incoming + state_total
    beyond = jnp.sum(state_end * after, axis=-1)
    upper = jnp.transpose(causal_mask(tokens))
    suffix = jnp.einsum("ij,sjc->sic", upper, grad_running, precision=HIGH)
    grad_log = suffix + beyond[:, None]
    grad_act = jnp.concatenate(
        [
            grad_query.reshape(seqs, tokens, key_dim) * root,
            grad_keys.reshape(seqs, tokens, key_dim),
            grad_values.reshape(seqs, tokens, value_dim),
        ],
        axis=-1,
    )
    grad_filtered = grad_act * silu_grad(filtered)
    later = shifted(grad_filtered[:, :lags], "seq", -1)
    padded_back = jnp.concatenate([grad_filtered, later], axis=1)
    grad_projected = taps[0] * grad_filtered
    tap_rows = [jnp.sum(grad_filtered * projected, axis=(0, 1))]
    for lag in range(1, lags + 1):
        grad_projected = grad_projected + taps[lag] * padded_back[:, lag : lag + tokens]
        tap_rows.append(
            jnp.sum(grad_filtered * padded[:, lags - lag : lags - lag + tokens], axis=(0, 1))
        )
    grad_taps = jnp.stack(tap_rows).reshape(lags + 1, 1, mixed_dim)
    grad_projected = grad_projected.reshape(total_rows, mixed_dim).astype(jnp.bfloat16)
    grad_logits = grad_log.reshape(total_rows, key_dim) * jax.nn.sigmoid(-logits) / NORMALIZER
    grad_bias = jnp.sum(grad_logits, axis=0)
    logits_low = grad_logits.astype(jnp.bfloat16)
    grad_expand = across(squeezed, logits_low)
    squeeze_low = against(logits_low, expand).astype(jnp.bfloat16)
    grad_squeeze = across(normed_one, squeeze_low)
    grad_project = across(normed_one, grad_projected).reshape(width, 1, mixed_dim)
    grad_gating = across(normed_one, grad_gatein)
    partial_value = (
        against(grad_projected, weight_in)
        + against(grad_gatein, gating)
        + against(squeeze_low, squeeze)
    )
    grad_one = lax.psum(partial_value, "head")
    grad_first = jnp.sum(grad_one * residual_in * scale_one, axis=0)
    input_grad = (grad_resid + rms_back(residual_in, scale_one, first_gain, grad_one)).reshape(
        seqs, tokens, width
    )
    mixer_grads = (
        lax.psum_scatter(grad_project, "seq", scatter_dimension=0, tiled=True),
        lax.psum_scatter(grad_gating, "seq", scatter_dimension=0, tiled=True),
        lax.psum_scatter(grad_output, "seq", scatter_dimension=1, tiled=True),
    )
    summed = tuple(mixer_grads) + tuple(feed_grads)
    small_head = lax.psum((grad_taps, grad_expand, grad_bias, grad_first, grad_second), "seq")
    shared = lax.psum((grad_scale, grad_squeeze), ("seq", "head"))
    return (
        block_out,
        input_grad,
        small_head[3],
        summed[0],
        small_head[0],
        shared[1],
        small_head[1],
        small_head[2],
        summed[1],
        shared[0],
        summed[2],
        small_head[4],
        summed[3],
        summed[4],
        summed[5],
    )


def solution(mesh):
    in_specs = (
        P(None, "seq", None),
        P(None, "seq", None),
        P(),
        P(None, "head", None),
        P(None, "head", None),
        P(),
        P(None, "head"),
        P("head"),
        P(None, "head"),
        P(),
        P("head", None),
        P(),
        P(None, "head"),
        P(None, "head"),
        P("head", None),
    )
    out_specs = (
        P(None, "seq", None),
        P(None, "seq", None),
        P(),
        P("seq", "head", None),
        P(None, "head", None),
        P(),
        P(None, "head"),
        P("head"),
        P("seq", "head"),
        P(),
        P("head", "seq"),
        P(),
        P("seq", "head"),
        P("seq", "head"),
        P("head", "seq"),
    )
    return jax.shard_map(body, mesh=mesh, in_specs=in_specs, out_specs=out_specs, check_vma=False)
```

profile of v0, /device:TPU:0, one launch (start us, length us, event | category | flops | bytes accessed | tf_op | source)
XLA Modules:
  0.0 871.2 jit_solution(14256679517528602044)
XLA Ops:
  7.3 1.3 fusion.21
  9.2 1.9 fusion.35
  11.2 4.9 collective-permute-start
  19.1 1.2 convolution_bitcast_fusion.2
  20.4 4.3 while.58
  26.0 21.5 %all-gather.3 = f32[8,1,128]{2,1,0:T(1,128)S(1)} all-gather(f32[1,1,128]{2,1,0:T(1,128)S(1)} %get-tuple-element.555), channel_id=2, replica_groups=mesh['seq'=8,'head'=4] {'seq'}, dimensions={0}, use_global_device_ids=true | all-gather | bytes 4608 | tf_op jit(solution)/shard_map/all_gather | solution.py:20
  49.4 18.3 %all-gather.7.cloned.1.call-done = f32[8,128,256]{2,1,0:T(8,128)} async-done(((f32[1,128,256]{2,1,0:T(8,128)}), f32[8,128,256]{2,1,0:T(8,128)}) %all-gather.7.cloned.1.call-update) | async-done | bytes 1048592 | tf_op jit(solution)/shard_map/all_gather | solution.py:20
  67.7 7.3 while.59
  75.6 1.6 multiply_reduce_fusion.7
  77.3 2.2 multiply_convert_fusion.6
  79.4 1.3 fusion.118
  80.8 35.1 %all-reduce.7.cloned.1.call-done = f32[256,1024]{1,0:T(8,128)} async-done(((f32[256,1024]{1,0:T(8,128)}), f32[256,1024]{1,0:T(8,128)}) %all-reduce.7.cloned.1.call-update) | async-done | bytes 1048592 | tf_op jit(solution)/shard_map/psum | solution.py:161
  115.9 1.4 multiply_reduce_fusion.2
  121.3 1.5 multiply_convert_fusion.1
  123.6 1.6 convolution_add_fusion.2
  125.3 1.2 multiply_multiply_fusion.1
  126.5 35.6 %all-reduce.9.cloned.1.call-done = f32[256,1024]{1,0:T(8,128)} async-done(((f32[256,1024]{1,0:T(8,128)}), f32[256,1024]{1,0:T(8,128)}) %all-reduce.9.cloned.1.call-update) | async-done | bytes 1048592 | tf_op jit(solution)/shard_map/psum | solution.py:182
  162.1 2.2 multiply_reduce_fusion
  165.6 1.6 fusion.65
  168.0 1.2 convolution_bitcast_fusion.1
  170.1 9.2 %while.60 = (s32[]{:T(128)}, f32[1,128,256]{2,1,0:T(8,128)S(1)}, f32[4,1,128,256]{3,2,1,0:T(8,128)}, f32[4,1,128]{2,1,0:T(1,128)}, f32[4,1,128,256]{3,2,1,0:T(8,128)}, /*index=5*/s32[]{:T(128)}, s32[]{:T(128)}, s32[]{:T(128)}) while((s32[]{:T(128)}, f32[1,128,256]{2,1,0:T(8,128)S(1)}, f32[4,1,128,256]{3,2,1,0:T(8,128)}, ...), condition=%wide.region_15.16_spmd.clone, body=%wide.region_14.15_spmd.clone.sunk | while | flops 131076 | bytes 657016 | solution.py:87
  180.9 2.6 fusion.121
  187.3 33.6 %all-gather.9.cloned.1.call-done = f32[8,128,256]{2,1,0:T(8,128)} async-done(((f32[1,128,256]{2,1,0:T(8,128)}), f32[8,128,256]{2,1,0:T(8,128)}) %all-gather.9.cloned.1.call-update) | async-done | bytes 1048592 | tf_op jit(solution)/shard_map/all_gather | solution.py:20
  220.9 2.3 reverse_bitcast_fusion
  223.2 15.3 %while.61 = (s32[]{:T(128)}, f32[1,128,256]{2,1,0:T(8,128)S(1)}, s32[]{:T(128)}, f32[8,1,128]{2,1,0:T(1,128)}, f32[8,1,128,256]{3,2,1,0:T(8,128)}, /*index=5*/s32[]{:T(128)}, s32[]{:T(128)}) while((s32[]{:T(128)}, f32[1,128,256]{2,1,0:T(8,128)S(1)}, s32[]{:T(128)}, f32[8,1,128]{2,1,0:T(1,128)}, f32[8,1,128,256]{3,2,1,0:T(8,128)}, ...), condition=%wide.region_17.18_spmd.clone, body=%wide.region_16.17_spmd.clone.sunk | while | flops 131076 | bytes 394857 | solution.py:32
  239.5 1.8 convolution_add_fusion.3
  243.0 1.4 collective-permute-start.1
  246.1 2.6 collective-permute-done.1
  250.2 1.3 convolution_add_fusion
  251.6 1.9 convolution_bitcast_fusion
  254.5 2.6 fusion.70
  257.2 2.4 fusion.105
  259.6 3.1 fusion.124
  262.8 3.2 fusion.125
  267.0 3.2 fusion.51
  270.8 38.8 %psum.86 = f32[256]{0:T(256)} all-reduce(f32[256]{0:T(256)S(1)} %copy-done.89), channel_id=1, replica_groups=mesh['seq'=8,'head'=4] {'seq','head'}, use_global_device_ids=true, to_apply=%region_35.36 | all-reduce | flops 256 | bytes 2048 | tf_op jit(solution)/shard_map/psum | solution.py:263
  309.9 1.5 fusion.30
  311.4 37.7 %all-reduce = (f32[1024]{0:T(1024)}, f32[4,1,512]{2,1,0:T(1,128)}, f32[16,128]{1,0:T(8,128)}, f32[128]{0:T(128)}, f32[1024]{0:T(1024)}) all-reduce(f32[1024]{0:T(1024)S(1)} %get-tuple-element.475, f32[4,1,512]{2,1,0:T(1,128)S(1)} %reshape.447, f32[16,128]{1,0:T(8,128)S(1)} %fusion.99, ...), channel_id=1, replica_groups=mesh['seq'=8,'head'=4] {'seq'}, use_global_device_ids=true, to_apply=%region_22.23 | all-reduce | flops 6272 | bytes 50176 | tf_op jit(solution)/shard_map/psum | solution.py:262
  349.1 3.4 fusion.27
  352.5 21.5 %reduce-scatter.7.cloned.1.call-done = f32[128,1,512]{2,0,1:T(8,128)} async-done(((f32[1024,1,512]{2,0,1:T(8,128)}), f32[128,1,512]{2,0,1:T(8,128)}) %reduce-scatter.7.cloned.1.call-update) | async-done | bytes 262160 | tf_op jit(solution)/shard_map/reduce_scatter | solution.py:257
  374.1 1.9 copy.47
  376.0 122.0 %all-reduce.11.cloned.1.call-done = f32[1024,16]{0,1:T(8,128)} async-done(((f32[1024,16]{0,1:T(8,128)}), f32[1024,16]{0,1:T(8,128)}) %all-reduce.11.cloned.1.call-update) | async-done | bytes 65552 | tf_op jit(solution)/shard_map/psum | solution.py:263
  498.0 69.9 %reduce-scatter.11.cloned.1.call-done = f32[256,128]{1,0:T(8,128)} async-done(((f32[256,1024]{1,0:T(8,128)}), f32[256,128]{1,0:T(8,128)}) %reduce-scatter.11.cloned.1.call-update) | async-done | bytes 131088 | tf_op jit(solution)/shard_map/reduce_scatter | solution.py:259
  567.9 67.2 %reduce-scatter.9.cloned.1.call-done = f32[128,256]{1,0:T(8,128)} async-done(((f32[1024,256]{1,0:T(8,128)}), f32[128,256]{1,0:T(8,128)}) %reduce-scatter.9.cloned.1.call-update) | async-done | bytes 131088 | tf_op jit(solution)/shard_map/reduce_scatter | solution.py:258
  635.2 75.6 %reduce-scatter.13.cloned.1.call-done = f32[128,704]{0,1:T(8,128)} async-done(((f32[1024,704]{0,1:T(8,128)}), f32[128,704]{0,1:T(8,128)}) %reduce-scatter.13.cloned.1.call-update) | async-done | bytes 360464 | tf_op jit(solution)/shard_map/reduce_scatter | solution.py:178
  710.8 76.2 %reduce-scatter.15.cloned.1.call-done = f32[128,704]{0,1:T(8,128)} async-done(((f32[1024,704]{0,1:T(8,128)}), f32[128,704]{0,1:T(8,128)}) %reduce-scatter.15.cloned.1.call-update) | async-done | bytes 360464 | tf_op jit(solution)/shard_map/reduce_scatter | solution.py:179
  787.0 75.9 %reduce-scatter.17.cloned.1.call-done = f32[704,128]{1,0:T(8,128)} async-done(((f32[704,1024]{1,0:T(8,128)}), f32[704,128]{1,0:T(8,128)}) %reduce-scatter.17.cloned.1.call-update) | async-done | bytes 360464 | tf_op jit(solution)/shard_map/reduce_scatter | solution.py:180
  862.9 1.5 copy.89
  (319 shorter events, 64.4 us)
Async XLA Ops:
  7.2 113.7 %copy-start = (bf16[704,1024]{1,0:T(8,128)(2,1)S(1)}, bf16[704,1024]{1,0:T(8,128)(2,1)}, u32[]{:S(2)}) copy-start(bf16[704,1024]{1,0:T(8,128)(2,1)} %param.37) | copy-start | bytes 4325380
  7.2 8.9 %copy-start.3 = (bf16[1,256,1024]{2,1,0:T(8,128)(2,1)S(1)}, bf16[1,256,1024]{2,1,0:T(8,128)(2,1)}, u32[]{:S(2)}) copy-start(bf16[1,256,1024]{2,1,0:T(8,128)(2,1)} %param.23) | copy-start | bytes 1572868
  7.2 8.9 %copy-start.53 = (f32[1024]{0:T(1024)S(1)}, f32[1024]{0:T(1024)}, u32[]{:S(2)}) copy-start(f32[1024]{0:T(1024)} %param.25) | copy-start | bytes 12292
  7.2 8.9 %copy-start.55 = (bf16[1024,16]{0,1:T(8,128)(2,1)S(1)}, bf16[1024,16]{0,1:T(8,128)(2,1)}, u32[]{:S(2)}) copy-start(bf16[1024,16]{0,1:T(8,128)(2,1)} %param.28) | copy-start | bytes 98308
  7.2 60.5 %all-gather.7.cloned.1.call-start = ((), (), s32[]{:S(2)}) async-start(), calls=%async_computation.15 | async-start | bytes 1179648 | tf_op jit(solution)/shard_map/all_gather | solution.py:20
  9.2 7.2 copy-start.83
  9.2 7.2 copy-start.91
  9.2 8.2 copy-start.81
  11.2 7.5 copy-start.8
  11.2 6.3 collective-permute-start
  18.7 49.0 %copy-start.12 = (f32[1,256,128]{2,1,0:T(8,128)}, f32[1,256,128]{2,1,0:T(8,128)S(1)}, u32[]{:S(2)}) copy-start(f32[1,256,128]{2,1,0:T(8,128)S(1)} %slice.81) | copy-start | bytes 393220
  18.8 29.7 %copy-start.19 = (bf16[1,256,256]{2,1,0:T(8,128)(2,1)}, bf16[1,256,256]{2,1,0:T(8,128)(2,1)S(1)}, u32[]{:S(2)}) copy-start(bf16[1,256,256]{2,1,0:T(8,128)(2,1)S(1)} %slice.82) | copy-start | bytes 393220
  19.1 148.3 %copy-start.24 = (f32[1,4,64,128]{3,2,1,0:T(8,128)}, f32[1,4,64,128]{3,2,1,0:T(8,128)S(1)}, u32[]{:S(2)}) copy-start(f32[1,4,64,128]{3,2,1,0:T(8,128)S(1)} %get-tuple-element.558) | copy-start | bytes 393220
  24.7 50.9 %copy-start.16 = (f32[4,1,128,256]{3,2,1,0:T(8,128)}, f32[4,1,128,256]{3,2,1,0:T(8,128)S(1)}, u32[]{:S(2)}) copy-start(f32[4,1,128,256]{3,2,1,0:T(8,128)S(1)} %get-tuple-element.335) | copy-start | bytes 1572868
  25.3 90.6 %all-reduce.7.cloned.1.call-start = ((), (), s32[]{:S(2)}) async-start(), calls=%async_computation.6 | async-start | bytes 2097152 | tf_op jit(solution)/shard_map/psum | solution.py:161
  25.4 42.3 %copy-start.47 = (f32[64,64]{1,0:T(8,128)}, f32[64,64]{1,0:T(8,128)S(1)}, u32[]{:S(2)}) copy-start(f32[64,64]{1,0:T(8,128)S(1)} %fusion.102) | copy-start | bytes 49156
  48.1 27.5 %copy-start.60 = (f32[4,128]{1,0:T(4,128)}, f32[4,128]{1,0:T(4,128)S(1)}, u32[]{:S(2)}) copy-start(f32[4,128]{1,0:T(4,128)S(1)} %get-tuple-element.549) | copy-start | bytes 6148
  48.5 28.7 %copy-start.34 = (f32[4,64,64]{2,1,0:T(8,128)}, f32[4,64,64]{2,1,0:T(8,128)S(1)}, u32[]{:S(2)}) copy-start(f32[4,64,64]{2,1,0:T(8,128)S(1)} %convolution_multiply_fusion.1) | copy-start | bytes 196612
  67.7 9.6 %copy-start.87 = (f32[256]{0:T(256)S(1)}, f32[256]{0:T(256)}, u32[]{:S(2)}) copy-start(f32[256]{0:T(256)} %param.32) | copy-start | bytes 3076
  80.7 37.2 %copy-start.54 = (f32[1024]{0:T(1024)S(1)}, f32[1024]{0:T(1024)}, u32[]{:S(2)}) copy-start(f32[1024]{0:T(1024)} %param.34) | copy-start | bytes 12292
  80.8 81.4 %all-reduce.9.cloned.1.call-start = ((), (), s32[]{:S(2)}) async-start(), calls=%async_computation.7 | async-start | bytes 2097152 | tf_op jit(solution)/shard_map/psum | solution.py:182
  125.2 95.7 %all-gather.9.cloned.1.call-start = ((), (), s32[]{:S(2)}) async-start(), calls=%async_computation.16 | async-start | bytes 1179648 | tf_op jit(solution)/shard_map/all_gather | solution.py:20
  170.1 10.1 %copy-start.73 = (f32[8,1,128]{2,1,0:T(1,128)S(1)}, f32[8,1,128]{2,1,0:T(1,128)}, u32[]{:S(2)}) copy-start(f32[8,1,128]{2,1,0:T(1,128)} %copy-done.72) | copy-start | bytes 12292
  180.0 129.8 %all-reduce.13.cloned.1.call-start = ((), (), s32[]{:S(2)}) async-start(), calls=%async_computation.17 | async-start | bytes 4194304 | tf_op jit(solution)/shard_map/psum | solution.py:168
  223.2 15.4 %copy-start.2 = (f32[1,128,256]{2,1,0:T(8,128)S(1)}, f32[1,128,256]{2,1,0:T(8,128)}, u32[]{:S(2)}) copy-start(f32[1,128,256]{2,1,0:T(8,128)} %copy-done.1) | copy-start | bytes 393220
  223.2 16.3 %copy-start.59 = (f32[4,128]{1,0:T(4,128)S(1)}, f32[4,128]{1,0:T(4,128)}, u32[]{:S(2)}) copy-start(f32[4,128]{1,0:T(4,128)} %get-tuple-element.548) | copy-start | bytes 6148
  242.0 4.0 copy-start.84
  242.0 6.7 copy-start.63
  242.0 6.7 copy-start.65
  242.0 6.7 copy-start.67
  242.0 6.7 copy-start.69
  243.0 5.9 copy-start.38
  243.0 5.7 collective-permute-start.1
  251.5 122.5 %reduce-scatter.7.cloned.1.call-start = ((), (), s32[]{:S(2)}) async-start(), calls=%async_computation.8 | async-start | bytes 2359296 | tf_op jit(solution)/shard_map/reduce_scatter | solution.py:257
  253.5 244.6 %all-reduce.11.cloned.1.call-start = ((), (), s32[]{:S(2)}) async-start(), calls=%async_computation.9 | async-start | bytes 131072 | tf_op jit(solution)/shard_map/psum | solution.py:263
  254.5 313.5 %reduce-scatter.11.cloned.1.call-start = ((), (), s32[]{:S(2)}) async-start(), calls=%async_computation.11 | async-start | bytes 1179648 | tf_op jit(solution)/shard_map/reduce_scatter | solution.py:259
  257.1 378.0 %reduce-scatter.9.cloned.1.call-start = ((), (), s32[]{:S(2)}) async-start(), calls=%async_computation.10 | async-start | bytes 1179648 | tf_op jit(solution)/shard_map/reduce_scatter | solution.py:258
  259.6 451.2 %reduce-scatter.13.cloned.1.call-start = ((), (), s32[]{:S(2)}) async-start(), calls=%async_computation.12 | async-start | bytes 3244032 | tf_op jit(solution)/shard_map/reduce_scatter | solution.py:178
  262.7 524.2 %reduce-scatter.15.cloned.1.call-start = ((), (), s32[]{:S(2)}) async-start(), calls=%async_computation.13 | async-start | bytes 3244032 | tf_op jit(solution)/shard_map/reduce_scatter | solution.py:179
  266.0 596.9 %reduce-scatter.17.cloned.1.call-start = ((), (), s32[]{:S(2)}) async-start(), calls=%async_computation.14 | async-start | bytes 3244032 | tf_op jit(solution)/shard_map/reduce_scatter | solution.py:180
  270.2 39.5 %copy-start.76 = (f32[512]{0:T(512)S(1)}, f32[512]{0:T(512)}, u32[]{:S(2)}) copy-start(f32[512]{0:T(512)} %get-tuple-element.478) | copy-start | bytes 6148
  270.2 39.5 %copy-start.77 = (f32[512]{0:T(512)S(1)}, f32[512]{0:T(512)}, u32[]{:S(2)}) copy-start(f32[512]{0:T(512)} %get-tuple-element.479) | copy-start | bytes 6148
  270.2 39.5 %copy-start.78 = (f32[512]{0:T(512)S(1)}, f32[512]{0:T(512)}, u32[]{:S(2)}) copy-start(f32[512]{0:T(512)} %get-tuple-element.482) | copy-start | bytes 6148
  270.2 39.5 %copy-start.51 = (bf16[256,128]{1,0:T(8,128)(2,1)S(1)}, bf16[256,128]{1,0:T(8,128)(2,1)}, u32[]{:S(2)}) copy-start(bf16[256,128]{1,0:T(8,128)(2,1)} %copy-done.50) | copy-start | bytes 196612
  270.2 39.5 %copy-start.80 = (bf16[256,16]{0,1:T(8,128)(2,1)S(1)}, bf16[256,16]{0,1:T(8,128)(2,1)}, u32[]{:S(2)}) copy-start(bf16[256,16]{0,1:T(8,128)(2,1)} %copy-done.79) | copy-start | bytes 24580
  270.2 41.2 %copy-start.71 = (f32[1024]{0:T(1024)S(1)}, f32[1024]{0:T(1024)}, u32[]{:S(2)}) copy-start(f32[1024]{0:T(1024)} %get-tuple-element.473) | copy-start | bytes 12292
  270.2 41.2 %copy-start.90 = (f32[128]{0:T(128)S(1)}, f32[128]{0:T(128)}, u32[]{:S(2)}) copy-start(f32[128]{0:T(128)} %get-tuple-element.566) | copy-start | bytes 1540
  270.2 78.9 %copy-start.85 = (f32[256]{0:T(256)S(1)}, f32[256]{0:T(256)}, u32[]{:S(2)}) copy-start(f32[256]{0:T(256)} %get-tuple-element.550) | copy-start | bytes 3076
  (59 other events, 104.7 us)
Sparse Core Ops, SparseCore 0:
  25.4 42.2 all-gather.6
  80.9 34.9 all-reduce.6
  125.4 36.7 all-reduce.8
  180.1 40.7 all-gather.8
  251.6 50.4 all-reduce.12
  305.5 68.4 reduce-scatter.6
  379.6 118.3 all-reduce.10
  502.0 65.8 reduce-scatter.10
  571.9 63.1 reduce-scatter.8
  639.1 71.6 reduce-scatter.12
  714.9 71.9 reduce-scatter.14
  791.0 71.8 reduce-scatter.16
where the time goes:
time: 873 us; the launch traced here: 871 us
  waiting for transfers between devices  634 us (73%)
  blocking collectives  98 us (11%)
  matrix products  47.6 us (5%)
  other arithmetic  42.4 us (5%)
  local copies, waits for them, and re-layouts  26.4 us (3%)
  between operations  15.4 us (2%)
    psum x1, waiting for transfers between devices, body(): shared = lax.psum((grad_scale, grad_squeeze), ('seq', 'head'))  122 us
    reduce_scatter x1, waiting for transfers between devices, body(): lax.psum_scatter(grad_lift, 'seq', scatter_dimension=0, tiled=True)  76.2 us
    reduce_scatter x1, waiting for transfers between devices, body(): lax.psum_scatter(grad_drop, 'seq', scatter_dimension=1, tiled=True)  75.9 us
    reduce_scatter x1, waiting for transfers between devices, body(): lax.psum_scatter(grad_gate, 'seq', scatter_dimension=0, tiled=True)  75.6 us
    reduce_scatter x1, waiting for transfers between devices, body(): lax.psum_scatter(grad_output, 'seq', scatter_dimension=1, tiled=True)  69.9 us
    reduce_scatter x1, waiting for transfers between devices, body(): lax.psum_scatter(grad_gating, 'seq', scatter_dimension=0, tiled=True)  67.2 us
    all_gather x2, waiting for transfers between devices, entering(): pieces = jax.tree.map(lambda part: lax.all_gather(part, axis), value)  51.9 us
    psum x1, blocking collectives, body(): shared = lax.psum((grad_scale, grad_squeeze), ('seq', 'head'))  38.8 us
  transfers between devices with their start and end apart: 14, of which 12 were waited for; matrix products, arithmetic and copies ran while one was open for 4% of the time, Pallas kernels for 0%

commit v1 on v0

--- a/solution.py
+++ b/solution.py
@@ -260,7 +260,7 @@
     )
     summed = tuple(mixer_grads) + tuple(feed_grads)
     small_head = lax.psum((grad_taps, grad_expand, grad_bias, grad_first, grad_second), "seq")
-    shared = lax.psum((grad_scale, grad_squeeze), ("seq", "head"))
+    shared = lax.psum(lax.psum((grad_scale, grad_squeeze), "head"), "seq")
     return (
         block_out,
         input_grad,

time: 873 us -> 822 us (0.942)
  blocking collectives: 98 us -> 65.3 us
  waiting for transfers between devices: 634 us -> 615 us
    psum x1, waiting for transfers between devices: 122 us -> 71.6 us  [body(): shared = lax.psum(lax.psum((grad_scale, grad_squeeze), 'head'), 'seq')]
    psum x1, waiting for transfers between devices: 0.01 us -> 43.4 us  [body(): feed = lax.psum(product(inner, hidden_drop), 'head')]
    psum x1, blocking collectives: 38.8 us -> 6.03 us  [body(): shared = lax.psum(lax.psum((grad_scale, grad_squeeze), 'head'), 'seq')]
    reduce_scatter x1, waiting for transfers between devices: 21.5 us -> 11.7 us  [body(): lax.psum_scatter(grad_project, 'seq', scatter_dimension=0, tiled=True)]
  transfers between devices with their start and end apart: 14 -> 14, of which waited for: 12 -> 13; matrix products, arithmetic and copies ran while one was open for 4% -> 4% of each run, Pallas kernels for 0% -> 0%
where the time goes in v1:
time: 822 us; the launch traced here: 820 us
  waiting for transfers between devices  615 us (75%)
  blocking collectives  65.3 us (8%)
  matrix products  47.5 us (6%)
  other arithmetic  42.4 us (5%)
  local copies, waits for them, and re-layouts  27.2 us (3%)
  between operations  15.3 us (2%)
    reduce_scatter x1, waiting for transfers between devices, body(): lax.psum_scatter(grad_gate, 'seq', scatter_dimension=0, tiled=True)  76.9 us
    reduce_scatter x1, waiting for transfers between devices, body(): lax.psum_scatter(grad_drop, 'seq', scatter_dimension=1, tiled=True)  76.2 us
    reduce_scatter x1, waiting for transfers between devices, body(): lax.psum_scatter(grad_lift, 'seq', scatter_dimension=0, tiled=True)  76.1 us
    psum x1, waiting for transfers between devices, body(): shared = lax.psum(lax.psum((grad_scale, grad_squeeze), 'head'), 'seq')  71.6 us
    reduce_scatter x1, waiting for transfers between devices, body(): lax.psum_scatter(grad_gating, 'seq', scatter_dimension=0, tiled=True)  67.1 us
    reduce_scatter x1, waiting for transfers between devices, body(): lax.psum_scatter(grad_output, 'seq', scatter_dimension=1, tiled=True)  65.7 us
    all_gather x2, waiting for transfers between devices, entering(): pieces = jax.tree.map(lambda part: lax.all_gather(part, axis), value)  51.8 us
    psum x1, waiting for transfers between devices, body(): feed = lax.psum(product(inner, hidden_drop), 'head')  43.4 us
  transfers between devices with their start and end apart: 14, of which 13 were waited for; matrix products, arithmetic and copies ran while one was open for 4% of the time, Pallas kernels for 0%

profile of v1, /device:TPU:0, one launch (start us, length us, event | category | flops | bytes accessed | tf_op | source)
XLA Modules:
  0.0 820.2 jit_solution(11301531786532587570)
XLA Ops:
  7.3 1.3 fusion.21
  9.2 1.9 fusion.35
  11.1 4.9 collective-permute-start
  19.0 1.2 convolution_bitcast_fusion.2
  20.3 4.3 while.58
  25.9 21.5 %all-gather.3 = f32[8,1,128]{2,1,0:T(1,128)S(1)} all-gather(f32[1,1,128]{2,1,0:T(1,128)S(1)} %get-tuple-element.557), channel_id=2, replica_groups=mesh['seq'=8,'head'=4] {'seq'}, dimensions={0}, use_global_device_ids=true | all-gather | bytes 4608 | tf_op jit(solution)/shard_map/all_gather | solution.py:20
  49.4 18.3 %all-gather.7.cloned.1.call-done = f32[8,128,256]{2,1,0:T(8,128)} async-done(((f32[1,128,256]{2,1,0:T(8,128)}), f32[8,128,256]{2,1,0:T(8,128)}) %all-gather.7.cloned.1.call-update) | async-done | bytes 1048592 | tf_op jit(solution)/shard_map/all_gather | solution.py:20
  67.7 7.3 while.59
  75.5 1.6 multiply_reduce_fusion.7
  77.2 2.2 multiply_convert_fusion.6
  79.4 1.3 fusion.118
  80.8 35.1 %all-reduce.7.cloned.1.call-done = f32[256,1024]{1,0:T(8,128)} async-done(((f32[256,1024]{1,0:T(8,128)}), f32[256,1024]{1,0:T(8,128)}) %all-reduce.7.cloned.1.call-update) | async-done | bytes 1048592 | tf_op jit(solution)/shard_map/psum | solution.py:161
  115.8 1.4 multiply_reduce_fusion.2
  121.2 1.5 multiply_convert_fusion.1
  123.6 1.6 convolution_add_fusion.2
  126.4 35.7 %all-reduce.9.cloned.1.call-done = f32[256,1024]{1,0:T(8,128)} async-done(((f32[256,1024]{1,0:T(8,128)}), f32[256,1024]{1,0:T(8,128)}) %all-reduce.9.cloned.1.call-update) | async-done | bytes 1048592 | tf_op jit(solution)/shard_map/psum | solution.py:182
  162.1 2.2 multiply_reduce_fusion
  165.5 1.6 fusion.65
  168.0 1.2 convolution_bitcast_fusion.1
  170.0 9.4 %while.60 = (s32[]{:T(128)}, f32[1,128,256]{2,1,0:T(8,128)S(1)}, f32[4,1,128,256]{3,2,1,0:T(8,128)}, f32[4,1,128]{2,1,0:T(1,128)}, f32[4,1,128,256]{3,2,1,0:T(8,128)}, /*index=5*/s32[]{:T(128)}, s32[]{:T(128)}, s32[]{:T(128)}) while((s32[]{:T(128)}, f32[1,128,256]{2,1,0:T(8,128)S(1)}, f32[4,1,128,256]{3,2,1,0:T(8,128)}, ...), condition=%wide.region_15.16_spmd.clone, body=%wide.region_14.15_spmd.clone.sunk | while | flops 131076 | bytes 657016 | solution.py:87
  181.0 2.7 fusion.121
  187.4 33.6 %all-gather.9.cloned.1.call-done = f32[8,128,256]{2,1,0:T(8,128)} async-done(((f32[1,128,256]{2,1,0:T(8,128)}), f32[8,128,256]{2,1,0:T(8,128)}) %all-gather.9.cloned.1.call-update) | async-done | bytes 1048592 | tf_op jit(solution)/shard_map/all_gather | solution.py:20
  221.0 2.3 reverse_bitcast_fusion
  223.3 15.3 %while.61 = (s32[]{:T(128)}, f32[1,128,256]{2,1,0:T(8,128)S(1)}, s32[]{:T(128)}, f32[8,1,128]{2,1,0:T(1,128)}, f32[8,1,128,256]{3,2,1,0:T(8,128)}, /*index=5*/s32[]{:T(128)}, s32[]{:T(128)}) while((s32[]{:T(128)}, f32[1,128,256]{2,1,0:T(8,128)S(1)}, s32[]{:T(128)}, f32[8,1,128]{2,1,0:T(1,128)}, f32[8,1,128,256]{3,2,1,0:T(8,128)}, ...), condition=%wide.region_17.18_spmd.clone, body=%wide.region_16.17_spmd.clone.sunk | while | flops 131076 | bytes 394857 | solution.py:32
  239.6 1.7 convolution_add_fusion.3
  244.5 1.4 collective-permute-start.1
  246.9 3.3 collective-permute-done.1
  251.7 1.3 convolution_add_fusion
  253.1 1.9 convolution_bitcast_fusion
  255.9 2.5 fusion.70
  258.5 2.4 fusion.105
  261.0 43.4 %all-reduce.13.cloned.1.call-done = (f32[256,1024]{1,0:T(8,128)}, f32[256,1024]{1,0:T(8,128)}, f32[1024,16]{0,1:T(8,128)}) async-done(((f32[256,1024]{1,0:T(8,128)}, f32[256,1024]{1,0:T(8,128)}, f32[1024,16]{0,1:T(8,128)}), (f32[256,1024]{1,0:T(8,128)}, f32[256,1024]{1,0:T(8,128)}, f32[1024,16]{0,1:T(8,128)})) %all-reduce.13.cloned.1.call-update) | async-done | bytes 2162704 | tf_op jit(solution)/shard_map/psum | solution.py:168
  304.5 3.1 fusion.124
  307.6 3.1 fusion.125
  311.8 3.2 fusion.51
  315.6 6.0 psum.101
  321.9 1.5 fusion.30
  323.4 37.7 %all-reduce = (f32[1024]{0:T(1024)}, f32[4,1,512]{2,1,0:T(1,128)}, f32[16,128]{1,0:T(8,128)}, f32[128]{0:T(128)}, f32[256]{0:T(256)}, /*index=5*/f32[1024]{0:T(1024)}) all-reduce(f32[1024]{0:T(1024)S(1)} %get-tuple-element.475, f32[4,1,512]{2,1,0:T(1,128)S(1)} %reshape.447, ...), channel_id=1, replica_groups=mesh['seq'=8,'head'=4] {'seq'}, use_global_device_ids=true, to_apply=%region_22.23 | all-reduce | flops 6528 | bytes 52224 | tf_op jit(solution)/shard_map/psum | solution.py:262
  361.1 3.5 fusion.27
  364.6 11.7 %reduce-scatter.7.cloned.1.call-done = f32[128,1,512]{2,0,1:T(8,128)} async-done(((f32[1024,1,512]{2,0,1:T(8,128)}), f32[128,1,512]{2,0,1:T(8,128)}) %reduce-scatter.7.cloned.1.call-update) | async-done | bytes 262160 | tf_op jit(solution)/shard_map/reduce_scatter | solution.py:257
  376.3 1.9 copy.47
  378.3 65.7 %reduce-scatter.11.cloned.1.call-done = f32[256,128]{1,0:T(8,128)} async-done(((f32[256,1024]{1,0:T(8,128)}), f32[256,128]{1,0:T(8,128)}) %reduce-scatter.11.cloned.1.call-update) | async-done | bytes 131088 | tf_op jit(solution)/shard_map/reduce_scatter | solution.py:259
  444.0 67.1 %reduce-scatter.9.cloned.1.call-done = f32[128,256]{1,0:T(8,128)} async-done(((f32[1024,256]{1,0:T(8,128)}), f32[128,256]{1,0:T(8,128)}) %reduce-scatter.9.cloned.1.call-update) | async-done | bytes 131088 | tf_op jit(solution)/shard_map/reduce_scatter | solution.py:258
  511.1 71.6 %all-reduce.11.cloned.1.call-done = f32[1024,16]{0,1:T(8,128)} async-done(((f32[1024,16]{0,1:T(8,128)}), f32[1024,16]{0,1:T(8,128)}) %all-reduce.11.cloned.1.call-update) | async-done | bytes 65552 | tf_op jit(solution)/shard_map/psum | solution.py:263
  582.8 76.9 %reduce-scatter.13.cloned.1.call-done = f32[128,704]{0,1:T(8,128)} async-done(((f32[1024,704]{0,1:T(8,128)}), f32[128,704]{0,1:T(8,128)}) %reduce-scatter.13.cloned.1.call-update) | async-done | bytes 360464 | tf_op jit(solution)/shard_map/reduce_scatter | solution.py:178
  659.6 76.1 %reduce-scatter.15.cloned.1.call-done = f32[128,704]{0,1:T(8,128)} async-done(((f32[1024,704]{0,1:T(8,128)}), f32[128,704]{0,1:T(8,128)}) %reduce-scatter.15.cloned.1.call-update) | async-done | bytes 360464 | tf_op jit(solution)/shard_map/reduce_scatter | solution.py:179
  735.7 76.2 %reduce-scatter.17.cloned.1.call-done = f32[704,128]{1,0:T(8,128)} async-done(((f32[704,1024]{1,0:T(8,128)}), f32[704,128]{1,0:T(8,128)}) %reduce-scatter.17.cloned.1.call-update) | async-done | bytes 360464 | tf_op jit(solution)/shard_map/reduce_scatter | solution.py:180
  811.9 1.5 copy.90
  (319 shorter events, 66.4 us)
Async XLA Ops:
  7.2 113.6 %copy-start = (bf16[704,1024]{1,0:T(8,128)(2,1)S(1)}, bf16[704,1024]{1,0:T(8,128)(2,1)}, u32[]{:S(2)}) copy-start(bf16[704,1024]{1,0:T(8,128)(2,1)} %param.37) | copy-start | bytes 4325380
  7.2 8.8 %copy-start.3 = (bf16[1,256,1024]{2,1,0:T(8,128)(2,1)S(1)}, bf16[1,256,1024]{2,1,0:T(8,128)(2,1)}, u32[]{:S(2)}) copy-start(bf16[1,256,1024]{2,1,0:T(8,128)(2,1)} %param.23) | copy-start | bytes 1572868
  7.2 8.8 %copy-start.53 = (f32[1024]{0:T(1024)S(1)}, f32[1024]{0:T(1024)}, u32[]{:S(2)}) copy-start(f32[1024]{0:T(1024)} %param.25) | copy-start | bytes 12292
  7.2 8.8 %copy-start.55 = (bf16[1024,16]{0,1:T(8,128)(2,1)S(1)}, bf16[1024,16]{0,1:T(8,128)(2,1)}, u32[]{:S(2)}) copy-start(bf16[1024,16]{0,1:T(8,128)(2,1)} %param.28) | copy-start | bytes 98308
  7.2 60.4 %all-gather.7.cloned.1.call-start = ((), (), s32[]{:S(2)}) async-start(), calls=%async_computation.15 | async-start | bytes 1179648 | tf_op jit(solution)/shard_map/all_gather | solution.py:20
  9.2 7.2 copy-start.83
  9.2 7.2 copy-start.91
  9.2 8.2 copy-start.81
  11.1 7.4 copy-start.8
  11.1 6.3 collective-permute-start
  18.7 49.0 %copy-start.12 = (f32[1,256,128]{2,1,0:T(8,128)}, f32[1,256,128]{2,1,0:T(8,128)S(1)}, u32[]{:S(2)}) copy-start(f32[1,256,128]{2,1,0:T(8,128)S(1)} %slice.81) | copy-start | bytes 393220
  18.7 29.7 %copy-start.19 = (bf16[1,256,256]{2,1,0:T(8,128)(2,1)}, bf16[1,256,256]{2,1,0:T(8,128)(2,1)S(1)}, u32[]{:S(2)}) copy-start(bf16[1,256,256]{2,1,0:T(8,128)(2,1)S(1)} %slice.82) | copy-start | bytes 393220
  19.0 148.3 %copy-start.24 = (f32[1,4,64,128]{3,2,1,0:T(8,128)}, f32[1,4,64,128]{3,2,1,0:T(8,128)S(1)}, u32[]{:S(2)}) copy-start(f32[1,4,64,128]{3,2,1,0:T(8,128)S(1)} %get-tuple-element.560) | copy-start | bytes 393220
  24.6 50.9 %copy-start.16 = (f32[4,1,128,256]{3,2,1,0:T(8,128)}, f32[4,1,128,256]{3,2,1,0:T(8,128)S(1)}, u32[]{:S(2)}) copy-start(f32[4,1,128,256]{3,2,1,0:T(8,128)S(1)} %get-tuple-element.335) | copy-start | bytes 1572868
  25.3 90.6 %all-reduce.7.cloned.1.call-start = ((), (), s32[]{:S(2)}) async-start(), calls=%async_computation.6 | async-start | bytes 2097152 | tf_op jit(solution)/shard_map/psum | solution.py:161
  25.3 42.3 %copy-start.47 = (f32[64,64]{1,0:T(8,128)}, f32[64,64]{1,0:T(8,128)S(1)}, u32[]{:S(2)}) copy-start(f32[64,64]{1,0:T(8,128)S(1)} %fusion.102) | copy-start | bytes 49156
  48.1 27.5 %copy-start.60 = (f32[4,128]{1,0:T(4,128)}, f32[4,128]{1,0:T(4,128)S(1)}, u32[]{:S(2)}) copy-start(f32[4,128]{1,0:T(4,128)S(1)} %get-tuple-element.551) | copy-start | bytes 6148
  48.4 28.7 %copy-start.34 = (f32[4,64,64]{2,1,0:T(8,128)}, f32[4,64,64]{2,1,0:T(8,128)S(1)}, u32[]{:S(2)}) copy-start(f32[4,64,64]{2,1,0:T(8,128)S(1)} %convolution_multiply_fusion.1) | copy-start | bytes 196612
  67.6 9.6 %copy-start.87 = (f32[256]{0:T(256)S(1)}, f32[256]{0:T(256)}, u32[]{:S(2)}) copy-start(f32[256]{0:T(256)} %param.32) | copy-start | bytes 3076
  80.7 37.2 %copy-start.54 = (f32[1024]{0:T(1024)S(1)}, f32[1024]{0:T(1024)}, u32[]{:S(2)}) copy-start(f32[1024]{0:T(1024)} %param.34) | copy-start | bytes 12292
  80.7 81.4 %all-reduce.9.cloned.1.call-start = ((), (), s32[]{:S(2)}) async-start(), calls=%async_computation.7 | async-start | bytes 2097152 | tf_op jit(solution)/shard_map/psum | solution.py:182
  125.2 95.8 %all-gather.9.cloned.1.call-start = ((), (), s32[]{:S(2)}) async-start(), calls=%async_computation.16 | async-start | bytes 1179648 | tf_op jit(solution)/shard_map/all_gather | solution.py:20
  170.0 10.3 %copy-start.73 = (f32[8,1,128]{2,1,0:T(1,128)S(1)}, f32[8,1,128]{2,1,0:T(1,128)}, u32[]{:S(2)}) copy-start(f32[8,1,128]{2,1,0:T(1,128)} %copy-done.72) | copy-start | bytes 12292
  180.1 124.3 %all-reduce.13.cloned.1.call-start = ((), (), s32[]{:S(2)}) async-start(), calls=%async_computation.17 | async-start | bytes 4325376 | tf_op jit(solution)/shard_map/psum | solution.py:168
  223.3 15.4 %copy-start.2 = (f32[1,128,256]{2,1,0:T(8,128)S(1)}, f32[1,128,256]{2,1,0:T(8,128)}, u32[]{:S(2)}) copy-start(f32[1,128,256]{2,1,0:T(8,128)} %copy-done.1) | copy-start | bytes 393220
  223.3 16.3 %copy-start.59 = (f32[4,128]{1,0:T(4,128)S(1)}, f32[4,128]{1,0:T(4,128)}, u32[]{:S(2)}) copy-start(f32[4,128]{1,0:T(4,128)} %get-tuple-element.550) | copy-start | bytes 6148
  243.5 6.7 copy-start.63
  243.5 6.7 copy-start.65
  243.5 6.7 copy-start.67
  243.5 6.7 copy-start.69
  244.5 5.9 copy-start.38
  244.5 5.7 collective-permute-start.1
  253.1 123.3 %reduce-scatter.7.cloned.1.call-start = ((), (), s32[]{:S(2)}) async-start(), calls=%async_computation.8 | async-start | bytes 2359296 | tf_op jit(solution)/shard_map/reduce_scatter | solution.py:257
  255.0 189.0 %reduce-scatter.11.cloned.1.call-start = ((), (), s32[]{:S(2)}) async-start(), calls=%async_computation.11 | async-start | bytes 1179648 | tf_op jit(solution)/shard_map/reduce_scatter | solution.py:259
  258.4 46.0 %copy-start.6 = (bf16[256,1024]{1,0:T(8,128)(2,1)S(1)}, bf16[256,1024]{1,0:T(8,128)(2,1)}, u32[]{:S(2)}) copy-start(bf16[256,1024]{1,0:T(8,128)(2,1)} %copy-done.5) | copy-start | bytes 1572868
  258.5 252.7 %reduce-scatter.9.cloned.1.call-start = ((), (), s32[]{:S(2)}) async-start(), calls=%async_computation.10 | async-start | bytes 1179648 | tf_op jit(solution)/shard_map/reduce_scatter | solution.py:258
  260.9 321.8 %all-reduce.11.cloned.1.call-start = ((), (), s32[]{:S(2)}) async-start(), calls=%async_computation.9 | async-start | bytes 131072 | tf_op jit(solution)/shard_map/psum | solution.py:263
  304.4 355.2 %reduce-scatter.13.cloned.1.call-start = ((), (), s32[]{:S(2)}) async-start(), calls=%async_computation.12 | async-start | bytes 3244032 | tf_op jit(solution)/shard_map/reduce_scatter | solution.py:178
  307.6 428.2 %reduce-scatter.15.cloned.1.call-start = ((), (), s32[]{:S(2)}) async-start(), calls=%async_computation.13 | async-start | bytes 3244032 | tf_op jit(solution)/shard_map/reduce_scatter | solution.py:179
  310.8 501.1 %reduce-scatter.17.cloned.1.call-start = ((), (), s32[]{:S(2)}) async-start(), calls=%async_computation.14 | async-start | bytes 3244032 | tf_op jit(solution)/shard_map/reduce_scatter | solution.py:180
  315.0 6.7 copy-start.76
  315.0 6.7 copy-start.77
  315.0 6.7 copy-start.78
  315.0 6.8 copy-start.51
  315.0 6.7 copy-start.80
  315.0 8.4 %copy-start.71 = (f32[1024]{0:T(1024)S(1)}, f32[1024]{0:T(1024)}, u32[]{:S(2)}) copy-start(f32[1024]{0:T(1024)} %get-tuple-element.473) | copy-start | bytes 12292
  315.0 8.4 %copy-start.90 = (f32[128]{0:T(128)S(1)}, f32[128]{0:T(128)}, u32[]{:S(2)}) copy-start(f32[128]{0:T(128)} %get-tuple-element.568) | copy-start | bytes 1540
  315.1 46.1 %copy-start.85 = (f32[256]{0:T(256)S(1)}, f32[256]{0:T(256)}, u32[]{:S(2)}) copy-start(f32[256]{0:T(256)} %get-tuple-element.552) | copy-start | bytes 3076
  (59 other events, 103.7 us)
Sparse Core Ops, SparseCore 0:
  25.4 42.2 all-gather.6
  80.8 34.9 all-reduce.6
  125.3 36.7 all-reduce.8
  180.2 40.7 all-gather.8
  253.2 51.1 all-reduce.12
  307.8 68.5 reduce-scatter.6
  380.3 63.6 reduce-scatter.10
  448.0 63.0 reduce-scatter.8
  514.5 68.1 all-reduce.10
  586.7 72.8 reduce-scatter.12
  663.8 71.9 reduce-scatter.14
  739.7 72.1 reduce-scatter.16
